TPU v7x, 256 devices: a whole 4x4x8 slice. The times are simulated.
256 devices in a mesh: frame: 16 (over x_hi, z), head: 8 (over y, core), dp: 2 (over x_lo).
Axes of the slice: x: 4 (x_hi: 2, x_lo: 2; x = x_hi * 2 + x_lo), y: 4, z: 8, core: 2. Of those that a mesh axis runs over, the one named last changes fastest.
Arguments:
- clip: bfloat16 [2, 4096, 256], P('dp', 'frame'), may hold values from -40 to 40
- block_ids: int32 [2, 4096], P('dp'), may hold values from 0 to 63, never falling along the last dimension, each value on 1 to 128 neighbouring positions
- w_spatial: bfloat16 [9, 256, 256], replicated, may hold values from -0.125 to 0.125
- w_temporal: bfloat16 [3, 256, 256], replicated, may hold values from -0.21875 to 0.21875
- w_query: bfloat16 [256, 2048], P(None, 'head'), may hold values from -0.375 to 0.375
- w_key: bfloat16 [256, 2048], P(None, 'head'), may hold values from -0.375 to 0.375
- w_value: bfloat16 [256, 2048], P(None, 'head'), may hold values from -0.375 to 0.375
- w_out: bfloat16 [2048, 256], P('head'), may hold values from -0.125 to 0.125
- cotangent: bfloat16 [2, 4096, 256], P('dp', 'frame'), may hold values from -6 to 6
Outputs:
- grad_spatial: float32 [9, 256, 256], replicated
- grad_temporal: float32 [3, 256, 256], replicated
- grad_query: float32 [256, 2048], P(None, 'head')
- grad_key: float32 [256, 2048], P(None, 'head')
- grad_value: float32 [256, 2048], P(None, 'head')
- grad_out: float32 [2048, 256], P('head')
Inputs may be any that keep to these rules, and one draw needn't show every extreme that they name: `block_ids`: block numbers never fall along a clip's tokens; every block has 1 to (128) tokens.
All inputs are finite; a program needn't handle non-finite values.
Results may differ from a plain program's by a relative error of at most 0.04.
Values may be sent and summed in bfloat16 or wider, within the bound.
No kernel may reach another device: no remote copies, remote signals or barrier semaphores. Data moves between devices by JAX's collectives and lax.ppermute only.
A program may use at most 128 MiB of HBM per device.

v0:
```python
import jax
import jax.numpy as jnp
from jax import lax
from jax.sharding import PartitionSpec as P

HD = 128
SIDE = 8
NEG_FILL = -1e30


def with_halo(cells, sides, width):
    for axis, dim in sides:
        count = lax.axis_size(axis)
        ends = count - 1
        head = lax.slice_in_dim(cells, 0, width, axis=dim)
        tail = lax.slice_in_dim(cells, cells.shape[dim] - width, cells.shape[dim], axis=dim)
        cells = jnp.concatenate(
            [
                lax.ppermute(tail, axis, [(i, (i + 1) % count) for i in range(ends)]),
                cells,
                lax.ppermute(head, axis, [((i + 1) % count, i) for i in range(ends)]),
            ],
            axis=dim,
        )
    return cells


def spatial_taps(frame_grid, side):
    padded = jnp.pad(frame_grid, ((0, 0), (1, 1), (1, 1), (0, 0)))
    count = frame_grid.shape[0] * side * side
    width = frame_grid.shape[3]
    return [
        padded[:, row_off : row_off + side, col_off : col_off + side, :].reshape(count, width)
        for row_off in range(3)
        for col_off in range(3)
    ]


def silu_slope(pre_act):
    sigma = jax.nn.sigmoid(pre_act)
    return sigma * (1.0 + pre_act * (1.0 - sigma))


def frame_rims(field):
    return with_halo(field, (("frame", 0),), SIDE * SIDE)


def take_head(matrix, which_head):
    return matrix[:, which_head * HD : (which_head + 1) * HD]


def contract_rows(left, right):
    return lax.dot_general(
        left, right, (((0,), (0,)), ((), ())), preferred_element_type=jnp.float32
    )


def on_device(clip, block_ids, w_spatial, w_temporal, w_query, w_key, w_value, w_out, cotangent):
    frames_in = clip[0]
    upstream = cotangent[0]
    clip_blocks = block_ids[0]
    tok_local, channels = frames_in.shape
    frame_len = SIDE * SIDE
    scale = HD ** (-0.5)
    grid = frames_in.reshape(tok_local // frame_len, SIDE, SIDE, channels)
    taps = spatial_taps(grid, SIDE)
    pre_act = jnp.zeros((tok_local, channels), jnp.float32)
    for offset in range(9):
        pre_act = pre_act + jnp.dot(
            taps[offset], w_spatial[offset], preferred_element_type=jnp.float32
        )
    hidden = jax.nn.silu(pre_act).astype(jnp.bfloat16)
    hidden_rim = frame_rims(hidden)
    temporal = jnp.zeros((tok_local, channels), jnp.float32)
    for offset in range(3):
        temporal = temporal + jnp.dot(
            hidden_rim[offset * frame_len : offset * frame_len + tok_local],
            w_temporal[offset],
            preferred_element_type=jnp.float32,
        )
    features = temporal.astype(jnp.bfloat16)
    queries_local = jnp.dot(features, w_query, preferred_element_type=jnp.float32).astype(
        jnp.bfloat16
    )
    keys_local = jnp.dot(features, w_key, preferred_element_type=jnp.float32).astype(jnp.bfloat16)
    values_local = jnp.dot(features, w_value, preferred_element_type=jnp.float32).astype(
        jnp.bfloat16
    )
    keys_every, values_every = (
        lax.all_gather(keys_local, "frame", axis=0, tiled=True),
        lax.all_gather(values_local, "frame", axis=0, tiled=True),
    )
    first_row = lax.axis_index("frame") * tok_local
    grad_attended = jnp.dot(upstream, w_out.T, preferred_element_type=jnp.float32).astype(
        jnp.bfloat16
    )
    queries_held, grad_held = (queries_local, grad_attended)
    held_blocks = lax.dynamic_slice_in_dim(clip_blocks, first_row, tok_local)
    visible = clip_blocks[None, :] <= held_blocks[:, None]
    heads_here = queries_local.shape[1] // HD
    width_here = queries_local.shape[1]
    attended_parts, grad_query_parts, prob_list, score_grads, norm_list, delta_list = (
        [],
        [],
        [],
        [],
        [],
        [],
    )
    for which_head in range(heads_here):
        query_head = take_head(queries_held, which_head)
        key_head = take_head(keys_every, which_head)
        value_head = take_head(values_every, which_head)
        grad_head = take_head(grad_held, which_head)
        scores = jnp.dot(query_head, key_head.T, preferred_element_type=jnp.float32) * scale
        masked = jnp.where(visible, scores, NEG_FILL)
        top = jnp.max(masked, axis=1, keepdims=True)
        total = jnp.sum(jnp.where(visible, jnp.exp(masked - top), 0.0), axis=1, keepdims=True)
        log_norm = top + jnp.log(total)
        probs = jnp.where(visible, jnp.exp(masked - log_norm), 0.0)
        probs_low = probs.astype(jnp.bfloat16)
        attended = jnp.dot(probs_low, value_head, preferred_element_type=jnp.float32).astype(
            jnp.bfloat16
        )
        delta = jnp.sum(
            grad_head.astype(jnp.float32) * attended.astype(jnp.float32), axis=1, keepdims=True
        )
        grad_probs = jnp.dot(grad_head, value_head.T, preferred_element_type=jnp.float32)
        grad_scores = (probs * (grad_probs - delta) * scale).astype(jnp.bfloat16)
        grad_query_parts.append(
            jnp.dot(grad_scores, key_head, preferred_element_type=jnp.float32).astype(jnp.bfloat16)
        )
        attended_parts.append(attended)
        prob_list.append(probs_low)
        score_grads.append(grad_scores)
        norm_list.append(log_norm)
        delta_list.append(delta)
    attended_all = jnp.concatenate(attended_parts, axis=1)
    grad_queries = jnp.concatenate(grad_query_parts, axis=1)
    key_parts = []
    value_parts = []
    for which_head in range(heads_here):
        score_cols = score_grads[which_head]
        prob_cols = prob_list[which_head]
        key_parts.append(contract_rows(score_cols, take_head(queries_held, which_head)))
        value_parts.append(contract_rows(prob_cols, take_head(grad_held, which_head)))
    summed = lax.psum_scatter(
        jnp.concatenate(key_parts + value_parts, axis=1), "frame", scatter_dimension=0, tiled=True
    )
    grad_keys = summed[:, :width_here].astype(jnp.bfloat16)
    grad_values = summed[:, width_here:].astype(jnp.bfloat16)
    grad_wq_local = contract_rows(features, grad_queries)
    grad_wk_local = contract_rows(features, grad_keys)
    grad_wv_local = contract_rows(features, grad_values)
    grad_wo_local = contract_rows(attended_all, upstream)
    back_part = jnp.dot(grad_queries, w_query.T, preferred_element_type=jnp.float32)
    back_part = back_part + jnp.dot(grad_keys, w_key.T, preferred_element_type=jnp.float32)
    back_part = back_part + jnp.dot(grad_values, w_value.T, preferred_element_type=jnp.float32)
    head_sum = lax.psum(back_part, "head")
    grad_features = (head_sum + upstream.astype(jnp.float32)).astype(jnp.bfloat16)
    grad_rim = frame_rims(grad_features)
    grad_wt = jnp.stack(
        [
            contract_rows(
                hidden_rim[offset * frame_len : offset * frame_len + tok_local], grad_features
            )
            for offset in range(3)
        ]
    )
    grad_hidden = jnp.zeros((tok_local, channels), jnp.float32)
    for offset in range(3):
        grad_hidden = grad_hidden + jnp.dot(
            grad_rim[(2 - offset) * frame_len : (2 - offset) * frame_len + tok_local],
            w_temporal[offset].T,
            preferred_element_type=jnp.float32,
        )
    grad_pre = (grad_hidden * silu_slope(pre_act)).astype(jnp.bfloat16)
    grad_ws = jnp.stack([contract_rows(taps[offset], grad_pre) for offset in range(9)])
    totals = lax.psum(
        (grad_ws, grad_wt, grad_wq_local, grad_wk_local, grad_wv_local, grad_wo_local),
        ("frame", "dp"),
    )
    factor = float(lax.axis_size("dp") * lax.axis_size("frame") * tok_local) ** (-0.5)
    return (
        totals[0] * factor,
        totals[1] * factor,
        totals[2] * factor,
        totals[3] * factor,
        totals[4] * factor,
        totals[5] * factor,
    )


def solution(mesh):
    in_specs = (
        P("dp", "frame", None),
        P("dp", None),
        P(),
        P(),
        P(None, "head"),
        P(None, "head"),
        P(None, "head"),
        P("head", None),
        P("dp", "frame", None),
    )
    out_specs = (P(), P(), P(None, "head"), P(None, "head"), P(None, "head"), P("head", None))
    return jax.shard_map(
        on_device, mesh=mesh, in_specs=in_specs, out_specs=out_specs, check_vma=False
    )
```

profile of v0, /device:TPU:8, one launch (start us, length us, event | category | flops | bytes accessed | tf_op | source)
XLA Modules:
  0.0 700.0 jit_solution(11616659482293236148)
XLA Ops:
  7.2 1.9 pad_slice_fusion
  9.2 1.2 fusion.60
  10.4 1.1 convolution_add_fusion.11
  12.7 0.9 multiply_convert_fusion
  13.6 4.0 collective-permute-start
  17.6 1.3 collective-permute-start.1
  19.1 4.3 collective-permute-done.1
  23.8 0.8 convolution_convert_fusion.2
  24.8 1.7 convolution_convert_fusion
  26.6 0.9 convolution_convert_fusion.1
  27.7 85.4 %all-gather.3.cloned.1.call-done = bf16[4096,256]{1,0:T(8,128)(2,1)} async-done(((bf16[256,256]{1,0:T(8,128)(2,1)}), bf16[4096,256]{1,0:T(8,128)(2,1)}) %all-gather.3.cloned.1.call-update) | async-done | bytes 2097168 | tf_op jit(solution)/shard_map/all_gather | solution.py:90
  113.1 2.3 fusion.108
  115.4 0.9 fusion.109
  116.3 1.9 fusion.6
  118.7 2.4 fusion.9
  121.1 1.3 copy-done.1
  122.4 1.8 fusion.91
  124.2 1.8 fusion.94
  126.0 72.5 %all-gather.5.cloned.1.call-done = bf16[4096,256]{1,0:T(8,128)(2,1)} async-done(((bf16[256,256]{1,0:T(8,128)(2,1)}), bf16[4096,256]{1,0:T(8,128)(2,1)}) %all-gather.5.cloned.1.call-update) | async-done | bytes 2097168 | tf_op jit(solution)/shard_map/all_gather | solution.py:91
  198.4 2.8 convolution_convert_fusion.5
  201.3 2.9 multiply_reduce_fusion.1
  204.3 1.7 fusion.5
  206.5 1.7 copy-done.4
  208.1 1.7 fusion.4
  209.8 1.3 copy-done.2
  211.6 1.1 copy-done.7
  213.4 3.8 pad_maximum_fusion
  217.4 2.8 convolution_convert_fusion.6
  220.3 0.9 convolution_convert_fusion.4
  221.2 0.9 fusion.83
  222.4 0.9 fusion.35
  223.3 216.4 %reduce-scatter.2.cloned.1.call-done = f32[256,512]{0,1:T(8,128)} async-done(((f32[4096,512]{0,1:T(8,128)}), f32[256,512]{0,1:T(8,128)}) %reduce-scatter.2.cloned.1.call-update) | async-done | bytes 524304 | tf_op jit(solution)/shard_map/reduce_scatter | solution.py:147
  439.7 1.1 convert.4
  440.8 0.9 fusion.74
  442.0 0.9 convolution_add_fusion.1
  443.0 0.9 fusion.71
  443.9 60.5 %all-reduce.5.cloned.1.call-done = f32[256,256]{1,0:T(8,128)} async-done(((f32[256,256]{1,0:T(8,128)}), f32[256,256]{1,0:T(8,128)}) %all-reduce.5.cloned.1.call-update) | async-done | bytes 262160 | tf_op jit(solution)/shard_map/psum | solution.py:159
  504.4 1.0 add_convert_fusion
  505.8 1.3 collective-permute-start.2
  507.1 4.5 collective-permute-start.3
  512.2 0.9 pad_maximum_fusion.1
  515.8 1.4 copy-done.9
  517.3 168.9 %all-reduce.7.cloned.1.call-done = (f32[9,256,256]{2,1,0:T(8,128)}, f32[3,256,256]{2,1,0:T(8,128)}, f32[256,256]{1,0:T(8,128)}, f32[256,256]{1,0:T(8,128)}, f32[256,256]{1,0:T(8,128)}, /*index=5*/f32[256,256]{1,0:T(8,128)}) async-done(((f32[9,256,256]{2,1,0:T(8,128)}, f32[3,256,256]{2,1,0:T(8,128)}, f32[256,256]{1,0:T(8,128)}, f32[256,256]{1,0:T(8,128)}, f32[256,256]{1,0:T(8,128)}, ...) | async-done | bytes 4194320 | tf_op jit(solution)/shard_map/psum | solution.py:179
  686.1 3.4 broadcast_multiply_fusion
  689.5 0.7 broadcast_multiply_fusion.5
  690.3 0.7 broadcast_multiply_fusion.4
  691.0 0.7 broadcast_multiply_fusion.3
  692.5 0.9 broadcast_multiply_fusion.1
  (142 shorter events, 9.2 us)
Async XLA Ops:
  7.2 20.4 %copy-start = (bf16[256,256]{1,0:T(8,128)(2,1)S(1)}, bf16[256,256]{1,0:T(8,128)(2,1)}, u32[]{:S(2)}) copy-start(bf16[256,256]{1,0:T(8,128)(2,1)} %param.13) | copy-start | bytes 393220
  7.2 4.7 copy-start.14
  7.2 4.3 copy-start.19
  7.2 105.9 %all-gather.3.cloned.1.call-start = ((), (), s32[]{:S(2)}) async-start(), calls=%async_computation.1 | async-start | bytes 2228224 | tf_op jit(solution)/shard_map/all_gather | solution.py:90
  9.2 3.3 copy-start.15
  9.2 3.5 copy-start.30
  11.9 7.0 %copy-start.17 = (bf16[3,256,256]{2,1,0:T(8,128)(2,1)S(1)}, bf16[3,256,256]{2,1,0:T(8,128)(2,1)}, u32[]{:S(2)}) copy-start(bf16[3,256,256]{2,1,0:T(8,128)(2,1)} %param.12) | copy-start | bytes 1179652
  12.5 11.3 %copy-start.27 = (bf16[256,256]{1,0:T(8,128)(2,1)S(1)}, bf16[256,256]{1,0:T(8,128)(2,1)}, u32[]{:S(2)}) copy-start(bf16[256,256]{1,0:T(8,128)(2,1)} %param.14) | copy-start | bytes 393220
  12.7 13.9 %copy-start.42 = (s32[1,4096]{1,0:T(1,128)S(1)}, s32[1,4096]{1,0:T(1,128)}, u32[]{:S(2)}) copy-start(s32[1,4096]{1,0:T(1,128)} %param.10) | copy-start | bytes 49156
  12.7 13.9 %copy-start.13 = (bf16[1,256,256]{2,1,0:T(8,128)(2,1)S(1)}, bf16[1,256,256]{2,1,0:T(8,128)(2,1)}, u32[]{:S(2)}) copy-start(bf16[1,256,256]{2,1,0:T(8,128)(2,1)} %param.17) | copy-start | bytes 393220
  13.6 13.0 %copy-start.37 = (bf16[256,256]{1,0:T(8,128)(2,1)S(1)}, bf16[256,256]{1,0:T(8,128)(2,1)}, u32[]{:S(2)}) copy-start(bf16[256,256]{1,0:T(8,128)(2,1)} %param.16) | copy-start | bytes 393220
  13.6 10.0 %collective-permute-start = (bf16[64,256]{1,0:T(8,128)(2,1)S(1)}, bf16[64,256]{1,0:T(8,128)(2,1)S(1)}, u32[]{:S(2)}, u32[]{:S(2)}) collective-permute-start(bf16[64,256]{1,0:T(8,128)(2,1)S(1)} %get-tuple-element.18), channel_id=1, source_target_pairs={{0,16},{16,32},{32,48},{48,64},{64,80},{80,96},{96,112},{112,128},... | collective-permute-start | bytes 98312 | tf_op jit(solution)/shard_map/ppermute | solution.py:19
  17.6 5.8 collective-permute-start.1
  23.4 91.9 %copy-start.38 = (bf16[64,256]{1,0:T(8,128)(2,1)}, bf16[64,256]{1,0:T(8,128)(2,1)S(1)}, u32[]{:S(2)}) copy-start(bf16[64,256]{1,0:T(8,128)(2,1)S(1)} %collective-permute-done.1) | copy-start | bytes 98308
  23.6 91.7 %copy-start.40 = (bf16[64,256]{1,0:T(8,128)(2,1)}, bf16[64,256]{1,0:T(8,128)(2,1)S(1)}, u32[]{:S(2)}) copy-start(bf16[64,256]{1,0:T(8,128)(2,1)S(1)} %collective-permute-done) | copy-start | bytes 98308
  24.7 173.7 %all-gather.5.cloned.1.call-start = ((), (), s32[]{:S(2)}) async-start(), calls=%async_computation.2 | async-start | bytes 2228224 | tf_op jit(solution)/shard_map/all_gather | solution.py:91
  26.5 413.2 %reduce-scatter.2.cloned.1.call-start = ((), (), s32[]{:S(2)}) async-start(), calls=%async_computation.3 | async-start | bytes 8912896 | tf_op jit(solution)/shard_map/reduce_scatter | solution.py:147
  26.6 89.7 %copy-start.43 = (s32[1,256]{1,0:T(1,128)}, s32[1,256]{1,0:T(1,128)S(1)}, u32[]{:S(2)}) copy-start(s32[1,256]{1,0:T(1,128)S(1)} %constant_dynamic-slice_fusion) | copy-start | bytes 3076
  27.7 87.6 %copy-start.25 = (bf16[256,256]{1,0:T(8,128)(2,1)}, bf16[256,256]{1,0:T(8,128)(2,1)S(1)}, u32[]{:S(2)}) copy-start(bf16[256,256]{1,0:T(8,128)(2,1)S(1)} %convolution_convert_fusion.3) | copy-start | bytes 393220
  113.1 2.3 copy-start.10
  115.4 2.9 copy-start.5
  116.3 2.4 copy-start.3
  118.3 2.8 copy-start.45
  118.3 2.8 copy-start.47
  118.7 3.7 copy-start.20
  198.4 5.8 copy-start.6
  201.3 4.7 copy-start.23
  201.3 2.9 copy-start.12
  201.3 2.9 copy-start.21
  201.3 2.9 copy-start.44
  201.3 2.9 copy-start.48
  211.2 2.2 copy-start.8
  217.2 287.1 %all-reduce.5.cloned.1.call-start = ((), (), s32[]{:S(2)}) async-start(), calls=%async_computation.4 | async-start | bytes 524288 | tf_op jit(solution)/shard_map/psum | solution.py:159
  217.4 2.9 copy-start.11
  221.2 220.5 %copy-start.28 = (bf16[256,256]{1,0:T(8,128)(2,1)S(1)}, bf16[256,256]{1,0:T(8,128)(2,1)}, u32[]{:S(2)}) copy-start(bf16[256,256]{1,0:T(8,128)(2,1)} %param.14) | copy-start | bytes 393220
  221.2 220.8 %copy-start.29 = (bf16[256,256]{1,0:T(8,128)(2,1)S(1)}, bf16[256,256]{1,0:T(8,128)(2,1)}, u32[]{:S(2)}) copy-start(bf16[256,256]{1,0:T(8,128)(2,1)} %param.15) | copy-start | bytes 393220
  223.3 282.3 %copy-start.18 = (bf16[3,256,256]{2,1,0:T(8,128)(2,1)S(1)}, bf16[3,256,256]{2,1,0:T(8,128)(2,1)}, u32[]{:S(2)}) copy-start(bf16[3,256,256]{2,1,0:T(8,128)(2,1)} %param.12) | copy-start | bytes 1179652
  440.8 70.9 %copy-start.41 = (bf16[64,256]{1,0:T(8,128)(2,1)S(1)}, bf16[64,256]{1,0:T(8,128)(2,1)}, u32[]{:S(2)}) copy-start(bf16[64,256]{1,0:T(8,128)(2,1)} %copy-done.40) | copy-start | bytes 98308
  441.7 70.2 %copy-start.39 = (bf16[64,256]{1,0:T(8,128)(2,1)S(1)}, bf16[64,256]{1,0:T(8,128)(2,1)}, u32[]{:S(2)}) copy-start(bf16[64,256]{1,0:T(8,128)(2,1)} %copy-done.38) | copy-start | bytes 98308
  442.9 243.2 %all-reduce.7.cloned.1.call-start = ((), (), s32[]{:S(2)}) async-start(), calls=%async_computation.5 | async-start | bytes 8388608 | tf_op jit(solution)/shard_map/psum | solution.py:179
  443.9 69.6 %copy-start.49 = (f32[256,256]{1,0:T(8,128)S(1)}, f32[256,256]{1,0:T(8,128)}, u32[]{:S(2)}) copy-start(f32[256,256]{1,0:T(8,128)} %get-tuple-element.31) | copy-start | bytes 786436
  505.8 7.7 %collective-permute-start.2 = (bf16[64,256]{1,0:T(8,128)(2,1)S(1)}, bf16[64,256]{1,0:T(8,128)(2,1)S(1)}, u32[]{:S(2)}, u32[]{:S(2)}) collective-permute-start(bf16[64,256]{1,0:T(8,128)(2,1)S(1)} %get-tuple-element.16), channel_id=1, source_target_pairs={{16,0},{32,16},{48,32},{64,48},{80,64},{96,80},{112,96},{128,112},... | collective-permute-start | bytes 98312 | tf_op jit(solution)/shard_map/ppermute | solution.py:21
  507.1 6.1 collective-permute-start.3
  686.1 3.4 copy-start.35
  686.1 4.2 copy-start.34
  686.1 4.9 copy-start.33
  686.1 5.6 copy-start.32
  686.1 6.3 copy-start.22
  (11 other events, 19.5 us)
Sparse Core Ops, SparseCore 0:
  24.8 88.2 all-gather.2
  116.2 82.1 all-gather.4
  217.3 222.3 reduce-scatter.1
  443.1 61.2 all-reduce.4
  517.4 168.7 all-reduce.6
where the time goes:
time: 700 us
  waiting for transfers between devices  608 us (87%)
  matrix products  37.3 us (5%)
  other arithmetic  18.4 us (3%)
  between operations  14.7 us (2%)
  starting transfers between devices  11.5 us (2%)
  local copies, waits for them, and re-layouts  9.96 us (1%)
    reduce_scatter x1, waiting for transfers between devices, on_device(): lax.psum_scatter(jnp.concatenate(key_parts + value_parts, axis=1), 'frame...  216 us
    psum x1, waiting for transfers between devices, on_device(): lax.psum((grad_ws, grad_wt, grad_wq_local, grad_wk_local, grad_wv_local,...  169 us
    all_gather x1, waiting for transfers between devices, on_device(): lax.all_gather(keys_local, 'frame', axis=0, tiled=True)  85.4 us
    all_gather x1, waiting for transfers between devices, on_device(): lax.all_gather(values_local, 'frame', axis=0, tiled=True)  72.5 us
    psum x1, waiting for transfers between devices, on_device(): head_sum = lax.psum(back_part, 'head')  60.5 us
  transfers between devices with their start and end apart: 9, of which 7 were waited for; matrix products, arithmetic and copies ran while one was open for 3% of the time, Pallas kernels for 0%

commit v1 on v0

--- a/solution.py
+++ b/solution.py
@@ -156,7 +156,9 @@
     back_part = jnp.dot(grad_queries, w_query.T, preferred_element_type=jnp.float32)
     back_part = back_part + jnp.dot(grad_keys, w_key.T, preferred_element_type=jnp.float32)
     back_part = back_part + jnp.dot(grad_values, w_value.T, preferred_element_type=jnp.float32)
-    head_sum = lax.psum(back_part, "head")
+    head_sum = back_part
+    for hop in (1, 2, 4):
+        head_sum = head_sum + lax.ppermute(head_sum, "head", [(dev, dev ^ hop) for dev in range(8)])
     grad_features = (head_sum + upstream.astype(jnp.float32)).astype(jnp.bfloat16)
     grad_rim = frame_rims(grad_features)
     grad_wt = jnp.stack(

time: 700 us -> 656 us (0.937)
  waiting for transfers between devices: 608 us -> 560 us
    psum x1 -> x0, waiting for transfers between devices: 60.5 us -> none  [on_device(): head_sum = lax.psum(back_part, 'head')]
    ppermute x0 -> x3, waiting for transfers between devices: none -> 12.3 us  [on_device(): lax.ppermute(head_sum, 'head', [(dev, dev ^ hop) for dev in range(8)])]
  transfers between devices with their start and end apart: 9 -> 11, of which waited for: 7 -> 9; matrix products, arithmetic and copies ran while one was open for 3% -> 4% of each run, Pallas kernels for 0% -> 0%
where the time goes in v1:
time: 656 us; the launch traced here: 655 us
  waiting for transfers between devices  560 us (85%)
  matrix products  38.4 us (6%)
  other arithmetic  17.5 us (3%)
  between operations  14.7 us (2%)
  starting transfers between devices  14.6 us (2%)
  local copies, waits for them, and re-layouts  10.6 us (2%)
    reduce_scatter x1, waiting for transfers between devices, on_device(): lax.psum_scatter(jnp.concatenate(key_parts + value_parts, axis=1), 'frame...  218 us
    psum x1, waiting for transfers between devices, on_device(): lax.psum((grad_ws, grad_wt, grad_wq_local, grad_wk_local, grad_wv_local,...  167 us
    all_gather x1, waiting for transfers between devices, on_device(): lax.all_gather(keys_local, 'frame', axis=0, tiled=True)  85.4 us
    all_gather x1, waiting for transfers between devices, on_device(): lax.all_gather(values_local, 'frame', axis=0, tiled=True)  72.5 us
  transfers between devices with their start and end apart: 11, of which 9 were waited for; matrix products, arithmetic and copies ran while one was open for 4% of the time, Pallas kernels for 0%

profile of v1, /device:TPU:8, one launch (start us, length us, event | category | flops | bytes accessed | tf_op | source)
XLA Modules:
  0.0 655.4 jit_solution(4069861680038425393)
XLA Ops:
  7.2 1.9 pad_slice_fusion
  9.2 1.2 fusion.60
  10.4 1.1 convolution_add_fusion.11
  12.7 0.9 multiply_convert_fusion
  13.6 4.0 collective-permute-start
  17.6 1.3 collective-permute-start.1
  19.1 4.3 collective-permute-done.1
  23.8 0.8 convolution_convert_fusion.2
  24.8 1.7 convolution_convert_fusion
  26.6 0.9 convolution_convert_fusion.1
  27.7 85.4 %all-gather.3.cloned.1.call-done = bf16[4096,256]{1,0:T(8,128)(2,1)} async-done(((bf16[256,256]{1,0:T(8,128)(2,1)}), bf16[4096,256]{1,0:T(8,128)(2,1)}) %all-gather.3.cloned.1.call-update) | async-done | bytes 2097168 | tf_op jit(solution)/shard_map/all_gather | solution.py:90
  113.1 2.3 fusion.108
  115.4 0.9 fusion.109
  116.3 1.9 fusion.6
  118.7 2.4 fusion.9
  121.2 1.3 copy-done.1
  122.5 1.7 fusion.91
  124.2 1.7 fusion.94
  126.0 72.5 %all-gather.5.cloned.1.call-done = bf16[4096,256]{1,0:T(8,128)(2,1)} async-done(((bf16[256,256]{1,0:T(8,128)(2,1)}), bf16[4096,256]{1,0:T(8,128)(2,1)}) %all-gather.5.cloned.1.call-update) | async-done | bytes 2097168 | tf_op jit(solution)/shard_map/all_gather | solution.py:91
  198.4 2.8 convolution_convert_fusion.5
  201.3 2.9 multiply_reduce_fusion.1
  204.3 1.7 fusion.5
  206.5 1.7 copy-done.4
  208.1 1.7 fusion.4
  209.8 1.3 copy-done.2
  211.6 1.1 copy-done.7
  213.4 3.8 pad_maximum_fusion
  217.4 2.8 convolution_convert_fusion.6
  220.3 0.9 convolution_convert_fusion.4
  222.1 217.6 %reduce-scatter.2.cloned.1.call-done = f32[256,512]{0,1:T(8,128)} async-done(((f32[4096,512]{0,1:T(8,128)}), f32[256,512]{0,1:T(8,128)}) %reduce-scatter.2.cloned.1.call-update) | async-done | bytes 524304 | tf_op jit(solution)/shard_map/reduce_scatter | solution.py:147
  439.7 1.1 convert.4
  440.8 1.1 convolution_add_fusion.2
  441.9 1.1 convolution_add_fusion.1
  443.2 1.5 collective-permute-done.2
  445.5 0.9 fusion.83
  446.4 0.9 fusion.35
  447.3 5.9 collective-permute-done.3
  453.2 2.3 collective-permute-start.4
  455.6 0.9 fusion.74
  456.5 0.9 fusion.71
  457.4 4.9 collective-permute-done.4
  462.9 1.3 collective-permute-start.5
  464.2 4.5 collective-permute-start.6
  469.2 0.9 pad_maximum_fusion.1
  472.9 1.4 copy-done.9
  474.3 167.2 %all-reduce.4.cloned.1.call-done = (f32[9,256,256]{2,1,0:T(8,128)}, f32[3,256,256]{2,1,0:T(8,128)}, f32[256,256]{1,0:T(8,128)}, f32[256,256]{1,0:T(8,128)}, f32[256,256]{1,0:T(8,128)}, /*index=5*/f32[256,256]{1,0:T(8,128)}) async-done(((f32[9,256,256]{2,1,0:T(8,128)}, f32[3,256,256]{2,1,0:T(8,128)}, f32[256,256]{1,0:T(8,128)}, f32[256,256]{1,0:T(8,128)}, f32[256,256]{1,0:T(8,128)}, ...) | async-done | bytes 4194320 | tf_op jit(solution)/shard_map/psum | solution.py:181
  641.6 3.4 broadcast_multiply_fusion
  647.9 0.9 broadcast_multiply_fusion.1
  (151 shorter events, 12.7 us)
Async XLA Ops:
  7.2 20.4 %copy-start = (bf16[256,256]{1,0:T(8,128)(2,1)S(1)}, bf16[256,256]{1,0:T(8,128)(2,1)}, u32[]{:S(2)}) copy-start(bf16[256,256]{1,0:T(8,128)(2,1)} %param.13) | copy-start | bytes 393220
  7.2 4.7 copy-start.14
  7.2 4.3 copy-start.19
  7.2 105.9 %all-gather.3.cloned.1.call-start = ((), (), s32[]{:S(2)}) async-start(), calls=%async_computation.1 | async-start | bytes 2228224 | tf_op jit(solution)/shard_map/all_gather | solution.py:90
  9.2 3.3 copy-start.15
  9.2 3.5 copy-start.32
  11.9 7.0 %copy-start.17 = (bf16[3,256,256]{2,1,0:T(8,128)(2,1)S(1)}, bf16[3,256,256]{2,1,0:T(8,128)(2,1)}, u32[]{:S(2)}) copy-start(bf16[3,256,256]{2,1,0:T(8,128)(2,1)} %param.12) | copy-start | bytes 1179652
  12.5 11.3 %copy-start.31 = (bf16[256,256]{1,0:T(8,128)(2,1)S(1)}, bf16[256,256]{1,0:T(8,128)(2,1)}, u32[]{:S(2)}) copy-start(bf16[256,256]{1,0:T(8,128)(2,1)} %param.14) | copy-start | bytes 393220
  12.7 13.9 %copy-start.44 = (s32[1,4096]{1,0:T(1,128)S(1)}, s32[1,4096]{1,0:T(1,128)}, u32[]{:S(2)}) copy-start(s32[1,4096]{1,0:T(1,128)} %param.10) | copy-start | bytes 49156
  12.7 13.9 %copy-start.13 = (bf16[1,256,256]{2,1,0:T(8,128)(2,1)S(1)}, bf16[1,256,256]{2,1,0:T(8,128)(2,1)}, u32[]{:S(2)}) copy-start(bf16[1,256,256]{2,1,0:T(8,128)(2,1)} %param.17) | copy-start | bytes 393220
  13.6 13.0 %copy-start.39 = (bf16[256,256]{1,0:T(8,128)(2,1)S(1)}, bf16[256,256]{1,0:T(8,128)(2,1)}, u32[]{:S(2)}) copy-start(bf16[256,256]{1,0:T(8,128)(2,1)} %param.16) | copy-start | bytes 393220
  13.6 10.0 %collective-permute-start = (bf16[64,256]{1,0:T(8,128)(2,1)S(1)}, bf16[64,256]{1,0:T(8,128)(2,1)S(1)}, u32[]{:S(2)}, u32[]{:S(2)}) collective-permute-start(bf16[64,256]{1,0:T(8,128)(2,1)S(1)} %get-tuple-element.18), channel_id=1, source_target_pairs={{0,16},{16,32},{32,48},{48,64},{64,80},{80,96},{96,112},{112,128},... | collective-permute-start | bytes 98312 | tf_op jit(solution)/shard_map/ppermute | solution.py:19
  17.6 5.8 collective-permute-start.1
  23.4 91.9 %copy-start.40 = (bf16[64,256]{1,0:T(8,128)(2,1)}, bf16[64,256]{1,0:T(8,128)(2,1)S(1)}, u32[]{:S(2)}) copy-start(bf16[64,256]{1,0:T(8,128)(2,1)S(1)} %collective-permute-done.1) | copy-start | bytes 98308
  23.6 91.7 %copy-start.42 = (bf16[64,256]{1,0:T(8,128)(2,1)}, bf16[64,256]{1,0:T(8,128)(2,1)S(1)}, u32[]{:S(2)}) copy-start(bf16[64,256]{1,0:T(8,128)(2,1)S(1)} %collective-permute-done) | copy-start | bytes 98308
  24.7 173.7 %all-gather.5.cloned.1.call-start = ((), (), s32[]{:S(2)}) async-start(), calls=%async_computation.2 | async-start | bytes 2228224 | tf_op jit(solution)/shard_map/all_gather | solution.py:91
  26.5 413.2 %reduce-scatter.2.cloned.1.call-start = ((), (), s32[]{:S(2)}) async-start(), calls=%async_computation.3 | async-start | bytes 8912896 | tf_op jit(solution)/shard_map/reduce_scatter | solution.py:147
  26.6 89.7 %copy-start.45 = (s32[1,256]{1,0:T(1,128)}, s32[1,256]{1,0:T(1,128)S(1)}, u32[]{:S(2)}) copy-start(s32[1,256]{1,0:T(1,128)S(1)} %constant_dynamic-slice_fusion) | copy-start | bytes 3076
  27.7 87.6 %copy-start.29 = (bf16[256,256]{1,0:T(8,128)(2,1)}, bf16[256,256]{1,0:T(8,128)(2,1)S(1)}, u32[]{:S(2)}) copy-start(bf16[256,256]{1,0:T(8,128)(2,1)S(1)} %convolution_convert_fusion.3) | copy-start | bytes 393220
  115.4 2.9 copy-start.5
  118.3 2.8 copy-start.47
  118.7 3.8 copy-start.20
  198.4 5.8 copy-start.6
  201.3 4.7 copy-start.23
  201.3 2.9 copy-start.12
  201.3 2.9 copy-start.21
  201.3 2.9 copy-start.46
  201.3 2.9 copy-start.50
  217.2 424.3 %all-reduce.4.cloned.1.call-start = ((), (), s32[]{:S(2)}) async-start(), calls=%async_computation.4 | async-start | bytes 8388608 | tf_op jit(solution)/shard_map/psum | solution.py:181
  217.4 2.9 copy-start.11
  221.8 224.6 %copy-start.24 = (bf16[256,128]{0,1:T(8,128)(2,1)S(1)}, bf16[256,128]{0,1:T(8,128)(2,1)}, u32[]{:S(2)}) copy-start(bf16[256,128]{0,1:T(8,128)(2,1)} %copy-done.23) | copy-start | bytes 196612
  221.8 224.6 %copy-start.38 = (bf16[256,128]{0,1:T(8,128)(2,1)S(1)}, bf16[256,128]{0,1:T(8,128)(2,1)}, u32[]{:S(2)}) copy-start(bf16[256,128]{0,1:T(8,128)(2,1)} %get-tuple-element.36) | copy-start | bytes 196612
  222.1 223.4 %copy-start.26 = (bf16[256,128]{0,1:T(8,128)(2,1)S(1)}, bf16[256,128]{0,1:T(8,128)(2,1)}, u32[]{:S(2)}) copy-start(bf16[256,128]{0,1:T(8,128)(2,1)} %copy-done.25) | copy-start | bytes 196612
  222.1 223.4 %copy-start.28 = (bf16[256,128]{0,1:T(8,128)(2,1)S(1)}, bf16[256,128]{0,1:T(8,128)(2,1)}, u32[]{:S(2)}) copy-start(bf16[256,128]{0,1:T(8,128)(2,1)} %copy-done.27) | copy-start | bytes 196612
  443.1 1.6 collective-permute-start.2
  444.7 17.9 %copy-start.18 = (bf16[3,256,256]{2,1,0:T(8,128)(2,1)S(1)}, bf16[3,256,256]{2,1,0:T(8,128)(2,1)}, u32[]{:S(2)}) copy-start(bf16[3,256,256]{2,1,0:T(8,128)(2,1)} %param.12) | copy-start | bytes 1179652
  444.8 24.0 %copy-start.43 = (bf16[64,256]{1,0:T(8,128)(2,1)S(1)}, bf16[64,256]{1,0:T(8,128)(2,1)}, u32[]{:S(2)}) copy-start(bf16[64,256]{1,0:T(8,128)(2,1)} %copy-done.42) | copy-start | bytes 98308
  444.8 8.4 %collective-permute-start.3 = (f32[256,256]{1,0:T(8,128)S(1)}, f32[256,256]{1,0:T(8,128)S(1)}, u32[]{:S(2)}, u32[]{:S(2)}) collective-permute-start(f32[256,256]{1,0:T(8,128)S(1)} %add.113), channel_id=1, source_target_pairs={{0,4},{2,6},{4,0},{6,2},{8,12},{10,14},{12,8},{14,10},{1,5},{3,7},... | collective-permute-start | bytes 786440 | tf_op jit(solution)/shard_map/ppermute | solution.py:161
  446.4 22.6 %copy-start.41 = (bf16[64,256]{1,0:T(8,128)(2,1)S(1)}, bf16[64,256]{1,0:T(8,128)(2,1)}, u32[]{:S(2)}) copy-start(bf16[64,256]{1,0:T(8,128)(2,1)} %copy-done.40) | copy-start | bytes 98308
  453.2 9.1 %collective-permute-start.4 = (f32[256,256]{1,0:T(8,128)S(1)}, f32[256,256]{1,0:T(8,128)S(1)}, u32[]{:S(2)}, u32[]{:S(2)}) collective-permute-start(f32[256,256]{1,0:T(8,128)S(1)} %add.114), channel_id=1, source_target_pairs={{0,8},{2,10},{4,12},{6,14},{8,0},{10,2},{12,4},{14,6},{1,9},{3,11}... | collective-permute-start | bytes 786440 | tf_op jit(solution)/shard_map/ppermute | solution.py:161
  462.4 8.2 %copy-start.51 = (f32[256,256]{1,0:T(8,128)S(1)}, f32[256,256]{1,0:T(8,128)}, u32[]{:S(2)}) copy-start(f32[256,256]{1,0:T(8,128)} %get-tuple-element.31) | copy-start | bytes 786436
  462.9 7.7 %collective-permute-start.5 = (bf16[64,256]{1,0:T(8,128)(2,1)S(1)}, bf16[64,256]{1,0:T(8,128)(2,1)S(1)}, u32[]{:S(2)}, u32[]{:S(2)}) collective-permute-start(bf16[64,256]{1,0:T(8,128)(2,1)S(1)} %get-tuple-element.16), channel_id=1, source_target_pairs={{16,0},{32,16},{48,32},{64,48},{80,64},{96,80},{112,96},{128,112},... | collective-permute-start | bytes 98312 | tf_op jit(solution)/shard_map/ppermute | solution.py:21
  464.2 6.1 collective-permute-start.6
  641.5 3.4 copy-start.37
  641.5 4.2 copy-start.36
  641.5 4.9 copy-start.35
  641.6 5.6 copy-start.34
  641.6 6.3 copy-start.22
  (15 other events, 26.7 us)
Sparse Core Ops, SparseCore 0:
  24.8 88.2 all-gather.2
  116.2 82.1 all-gather.4
  217.3 222.3 reduce-scatter.1
  474.4 167.0 all-reduce.3
